TPU v7x, 32 devices: a whole 2x2x4 slice. The times are simulated.
32 devices in a mesh: groups: 1, tm: 32 (over z, y, x, core).
Axes of the slice: x: 2, y: 2, z: 4, core: 2. Of those that a mesh axis runs over, the one named last changes fastest.
Arguments:
- latents: bfloat16 [32, 512, 512], P(('groups', 'tm')), may hold values from -21 to 21
- w_query: bfloat16 [512, 512], replicated, may hold values from -3 to 3
- w_key: bfloat16 [512, 512], replicated, may hold values from -3 to 3
- w_value: bfloat16 [512, 512], replicated, may hold values from -0.25 to 0.25
- w_out: bfloat16 [512, 512], replicated, may hold values from -0.25 to 0.25
- w_time: bfloat16 [3, 512, 512], replicated, may hold values from -0.15625 to 0.15625
- w_space: bfloat16 [3, 3, 512, 512], replicated, may hold values from -0.09375 to 0.09375
- tile_starts: int32 [4], P('groups'), may hold values from 0 to 25, as said below
Outputs:
- decoded: bfloat16 [32, 512, 512], P(('groups', 'tm'))
Inputs may be any that keep to these rules, and one draw needn't show every extreme that they name: `tile_starts`: Increasing; the first is 0, the last is (3) * 8 + 1, and every other start t lies within 2 frames of t * 8.
All inputs are finite; a program needn't handle non-finite values.
Results may differ from a plain program's by a relative error of at most 0.0096.
Values may be sent and summed in bfloat16 or wider, within the bound.
A program may use at most 64 MiB of HBM per device.

v0:
```python
import jax
import jax.numpy as jnp
from jax import lax
from jax.sharding import PartitionSpec as P

PH = 16
PW = 32
OV = 2


epsilon = 1e-06


def passed_along(block, axis, distance):
    devices = range(lax.axis_size(axis))
    route = [(i - distance, i) for i in devices if i - distance in devices]
    return lax.ppermute(block, axis, route)


def rms_norm(array):
    wide = array.astype(jnp.float32)
    return (wide * lax.rsqrt(jnp.mean(wide * wide, axis=-1, keepdims=True) + epsilon)).astype(
        jnp.bfloat16
    )


def project(array, weight):
    extent = array.shape
    product = jnp.dot(array.reshape(-1, extent[-1]), weight, preferred_element_type=jnp.float32)
    return product.reshape(extent[:-1] + (weight.shape[-1],))


def tile_frames(frames, starts):
    reached = starts[None, :] <= frames[:, None]
    new_start = jnp.max(jnp.where(reached, starts[None, :], 0), axis=1)
    earlier = starts[None, :] < new_start[:, None]
    old_start = jnp.max(jnp.where(earlier, starts[None, :], 0), axis=1)
    inside = frames - new_start
    shared = jnp.logical_and(new_start > 0, inside < OV)
    fade = jnp.where(shared, (inside + 1).astype(jnp.float32) / float(OV + 1), jnp.float32(1.0))
    return (new_start, old_start, fade[:, None, None])


def attend(triple):
    queries, key_rows, values = triple
    length = queries.shape[0]
    scale = queries.shape[-1] ** (-0.5)
    scores = (
        jnp.einsum("fipc,gipc->ipfg", queries, key_rows, preferred_element_type=jnp.float32) * scale
    )
    order = jnp.arange(length)
    causal = order[:, None] >= order[None, :]
    scores = jnp.where(causal[None, None], scores, jnp.float32(-1e30))
    peak = jnp.max(scores, axis=-1, keepdims=True)
    expo = jnp.exp(scores - peak)
    weights = (expo / jnp.sum(expo, axis=-1, keepdims=True)).astype(jnp.bfloat16)
    return jnp.einsum(
        "ipfg,gipc->fipc", weights, values, preferred_element_type=jnp.float32
    ).astype(jnp.bfloat16)


def time_blend(padded, frames, starts, w_time):
    length = frames.shape[0]
    extent = padded.shape
    channels = extent[-1]
    flattened = padded.reshape(-1, channels)
    products = [
        jnp.dot(flattened, w_time[lag_index], preferred_element_type=jnp.float32).reshape(
            extent[0], -1, channels
        )
        for lag_index in range(3)
    ]
    new_start, old_start, fade = tile_frames(frames, starts)

    def mixed(context):
        summed = jnp.zeros((length,) + products[0].shape[1:], jnp.float32)
        for lag_index in range(3):
            actual = jnp.minimum(lag_index, frames - context)
            for delta_back in range(lag_index + 1):
                chosen = (actual == delta_back).astype(jnp.float32)[:, None, None]
                summed = (
                    summed + chosen * products[lag_index][2 - delta_back : 2 - delta_back + length]
                )
        return summed

    blended = fade * jax.nn.silu(mixed(new_start)) + (1.0 - fade) * jax.nn.silu(mixed(old_start))
    return blended.astype(jnp.bfloat16)


def space_mix(blended, hidden, w_space):
    length = blended.shape[0]
    channels = blended.shape[-1]
    spatial = blended.reshape(length, PH, PW, channels)
    padded = jnp.pad(spatial, ((0, 0), (1, 1), (1, 1), (0, 0)))
    summed = hidden.reshape(-1, channels).astype(jnp.float32)
    for row_shift in range(3):
        for col_shift in range(3):
            window = padded[:, row_shift : row_shift + PH, col_shift : col_shift + PW].reshape(
                -1, channels
            )
            summed = summed + jnp.dot(
                window, w_space[row_shift, col_shift], preferred_element_type=jnp.float32
            )
    return summed.reshape(length, PH * PW, channels).astype(jnp.bfloat16)


def body(latents, w_query, w_key, w_value, w_out, w_time, w_space, tile_starts):
    frames_dev, row_count, channels = latents.shape
    devices_tm = lax.axis_size("tm")
    share = row_count // devices_tm
    normed = rms_norm(latents).reshape(frames_dev, devices_tm, share, channels)
    queries = project(normed, w_query).astype(jnp.bfloat16)
    key_rows = project(normed, w_key).astype(jnp.bfloat16)
    values = project(normed, w_value).astype(jnp.bfloat16)
    attended = attend(
        (
            lax.all_to_all(queries, "tm", split_axis=1, concat_axis=0, tiled=True),
            lax.all_to_all(key_rows, "tm", split_axis=1, concat_axis=0, tiled=True),
            lax.all_to_all(values, "tm", split_axis=1, concat_axis=0, tiled=True),
        )
    )
    attended = lax.all_to_all(attended, "tm", split_axis=0, concat_axis=1, tiled=True).reshape(
        frames_dev, row_count, channels
    )
    hidden = (latents.astype(jnp.float32) + project(attended, w_out)).astype(jnp.bfloat16)
    smooth = rms_norm(hidden)
    reach = (frames_dev + 1) // frames_dev
    pieces = [passed_along(smooth, "tm", stride) for stride in range(reach, 0, -1)]
    earlier = jnp.concatenate(pieces, axis=0)
    offset = lax.axis_index("tm") * frames_dev
    frames = offset + jnp.arange(frames_dev)
    blended = time_blend(jnp.concatenate([earlier, smooth], axis=0), frames, tile_starts, w_time)
    return space_mix(blended, hidden, w_space)


def solution(mesh):
    placed = (P(("groups", "tm"), None, None), P(), P(), P(), P(), P(), P(), P("groups"))
    return jax.shard_map(
        body, mesh=mesh, in_specs=placed, out_specs=P(("groups", "tm"), None, None), check_vma=False
    )
```

profile of v0, /device:TPU:13, one launch (start us, length us, event | category | flops | bytes accessed | tf_op | source)
XLA Modules:
  0.0 115.6 jit_solution(4229719521326724587)
XLA Ops:
  0.0 1.3 %fusion.11 = f32[512]{0:T(512)S(1)} fusion(bf16[1,512,512]{2,1,0:T(8,128)(2,1)} %param.8), kind=kLoop, calls=%fused_computation.33 | loop fusion | flops 785920 | bytes 526336 | tf_op jit(solution)/shard_map/reduce_sum | solution.py:22
  1.3 1.3 %fusion.12 = bf16[1,512,512]{2,1,0:T(8,128)(2,1)S(1)} fusion(bf16[1,512,512]{2,1,0:T(8,128)(2,1)} %param.8, f32[512]{0:T(512)S(1)} %add_rsqrt_fusion.1), kind=kLoop, calls=%fused_computation.34 | loop fusion | flops 786432 | bytes 1050624 | tf_op jit(solution)/shard_map/convert_element_type | solution.py:22
  2.6 2.3 %fusion.7 = bf16[1,32,16,512]{3,2,0,1:T(8,128)(2,1)} fusion(bf16[32,16,512]{2,1,0:T(8,128)(2,1)S(1)} %bitcast.117, bf16[512,512]{1,0:T(8,128)(2,1)} %param.10), kind=kOutput, calls=%fused_computation.28 | convolution fusion | flops 268697600 | bytes 1572864 | tf_op jit(solution)/shard_map/dot_general | solution.py:29
  4.9 6.3 %all-to-all-start.2 = ((bf16[1,32,16,512]{3,2,0,1:T(8,128)(2,1)}), bf16[1,32,16,512]{3,2,0,1:T(8,128)(2,1)S(1)}, u32[]{:S(2)}, u32[]{:S(2)}) async-start(bf16[1,32,16,512]{3,2,0,1:T(8,128)(2,1)} %fusion.7), calls=%async_computation.2 | async-start | bytes 1048576 | tf_op jit(solution)/shard_map/all_to_all | solution.py:118
  11.2 1.2 %fusion.6 = bf16[1,32,16,512]{3,2,0,1:T(8,128)(2,1)} fusion(bf16[32,16,512]{2,1,0:T(8,128)(2,1)S(1)} %bitcast.118, bf16[512,512]{1,0:T(8,128)(2,1)S(1)} %copy-done.3), kind=kOutput, calls=%fused_computation.27 | convolution fusion | flops 268697600 | bytes 1572864 | tf_op jit(solution)/shard_map/dot_general | solution.py:29
  12.4 12.5 %all-to-all-done.2 = bf16[1,32,16,512]{3,2,0,1:T(8,128)(2,1)S(1)} async-done(((bf16[1,32,16,512]{3,2,0,1:T(8,128)(2,1)}), bf16[1,32,16,512]{3,2,0,1:T(8,128)(2,1)S(1)}, u32[]{:S(2)}, u32[]{:S(2)}) %all-to-all-start.2) | async-done | bytes 524320 | tf_op jit(solution)/shard_map/all_to_all | solution.py:118
  24.9 4.9 %all-to-all-start.1 = ((bf16[1,32,16,512]{3,2,0,1:T(8,128)(2,1)}), bf16[1,32,16,512]{3,2,0,1:T(8,128)(2,1)S(1)}, u32[]{:S(2)}, u32[]{:S(2)}) async-start(bf16[1,32,16,512]{3,2,0,1:T(8,128)(2,1)} %fusion.6), calls=%async_computation.1 | async-start | bytes 1048576 | tf_op jit(solution)/shard_map/all_to_all | solution.py:117
  29.8 1.2 %fusion.5 = bf16[1,32,16,512]{3,2,0,1:T(8,128)(2,1)} fusion(bf16[32,16,512]{2,1,0:T(8,128)(2,1)S(1)} %bitcast.119, bf16[512,512]{1,0:T(8,128)(2,1)S(1)} %copy-done.4), kind=kOutput, calls=%fused_computation.26 | convolution fusion | flops 268697600 | bytes 1572864 | tf_op jit(solution)/shard_map/dot_general | solution.py:29
  31.1 12.5 %all-to-all-done.1 = bf16[1,32,16,512]{3,2,0,1:T(8,128)(2,1)S(1)} async-done(((bf16[1,32,16,512]{3,2,0,1:T(8,128)(2,1)}), bf16[1,32,16,512]{3,2,0,1:T(8,128)(2,1)S(1)}, u32[]{:S(2)}, u32[]{:S(2)}) %all-to-all-start.1) | async-done | bytes 524320 | tf_op jit(solution)/shard_map/all_to_all | solution.py:117
  43.6 4.9 %all-to-all-start = ((bf16[1,32,16,512]{3,2,0,1:T(8,128)(2,1)}), bf16[1,32,16,512]{3,2,0,1:T(8,128)(2,1)S(1)}, u32[]{:S(2)}, u32[]{:S(2)}) async-start(bf16[1,32,16,512]{3,2,0,1:T(8,128)(2,1)} %fusion.5), calls=%async_computation | async-start | bytes 1048576 | tf_op jit(solution)/shard_map/all_to_all | solution.py:119
  48.5 0.7 fusion.57
  49.2 13.0 %all-to-all-done = bf16[1,32,16,512]{3,2,0,1:T(8,128)(2,1)S(1)} async-done(((bf16[1,32,16,512]{3,2,0,1:T(8,128)(2,1)}), bf16[1,32,16,512]{3,2,0,1:T(8,128)(2,1)S(1)}, u32[]{:S(2)}, u32[]{:S(2)}) %all-to-all-start) | async-done | bytes 524320 | tf_op jit(solution)/shard_map/all_to_all | solution.py:119
  63.0 18.4 %all_to_all.16 = bf16[32,1,16,512]{3,2,1,0:T(8,128)(2,1)S(1)} all-to-all(bf16[32,1,16,512]{3,2,1,0:T(8,128)(2,1)S(1)} %copy.25), channel_id=1, replica_groups=mesh['groups'=1,'tm'=32] {'tm'}, dimensions={0} | all-to-all | bytes 1048576 | tf_op jit(solution)/shard_map/all_to_all | solution.py:122
  82.2 3.0 %collective-permute-start.1 = (bf16[1,512,512]{2,1,0:T(8,128)(2,1)S(1)}, bf16[1,512,512]{2,1,0:T(8,128)(2,1)}, u32[]{:S(2)}, u32[]{:S(2)}) collective-permute-start(bf16[1,512,512]{2,1,0:T(8,128)(2,1)S(1)} %fusion.14), channel_id=1, source_target_pairs={{0,1},{1,2},{2,3},{3,4},{4,5},{5,6},{6,7},{7,8},{8,9},{9,10},{10,1... | collective-permute-start | bytes 1572872 | tf_op jit(solution)/shard_map/ppermute | solution.py:17
  85.3 2.9 %collective-permute-start = (bf16[1,512,512]{2,1,0:T(8,128)(2,1)S(1)}, bf16[1,512,512]{2,1,0:T(8,128)(2,1)}, u32[]{:S(2)}, u32[]{:S(2)}) collective-permute-start(bf16[1,512,512]{2,1,0:T(8,128)(2,1)S(1)} %fusion.14), channel_id=1, source_target_pairs={{0,2},{1,3},{2,4},{3,5},{4,6},{5,7},{6,8},{7,9},{8,10},{9,11},{10,... | collective-permute-start | bytes 1572872 | tf_op jit(solution)/shard_map/ppermute | solution.py:17
  88.8 1.2 %fusion.56 = s32[]{:T(128)} fusion(s32[4]{0:T(128)S(1)} %copy-done.5, s32[]{:T(128)} %fusion.55), kind=kLoop, calls=%fused_computation.91 | loop fusion | flops 11 | bytes 24 | tf_op jit(solution)/shard_map/reduce_max | solution.py:37
  92.0 2.4 %collective-permute-done.1 = bf16[1,512,512]{2,1,0:T(8,128)(2,1)} collective-permute-done((bf16[1,512,512]{2,1,0:T(8,128)(2,1)S(1)}, bf16[1,512,512]{2,1,0:T(8,128)(2,1)}, u32[]{:S(2)}, u32[]{:S(2)}) %collective-permute-start.1) | collective-permute-done | bytes 524320 | tf_op jit(solution)/shard_map/ppermute | solution.py:17
  94.4 10.8 %collective-permute-done = bf16[1,512,512]{2,1,0:T(8,128)(2,1)} collective-permute-done((bf16[1,512,512]{2,1,0:T(8,128)(2,1)S(1)}, bf16[1,512,512]{2,1,0:T(8,128)(2,1)}, u32[]{:S(2)}, u32[]{:S(2)}) %collective-permute-start) | collective-permute-done | bytes 524320 | tf_op jit(solution)/shard_map/ppermute | solution.py:17
  105.2 1.4 %pad_maximum_fusion = bf16[3,512,512]{2,1,0:T(8,128)(2,1)S(1)} fusion(bf16[1,512,512]{2,1,0:T(8,128)(2,1)S(1)} %fusion.14, bf16[1,512,512]{2,1,0:T(8,128)(2,1)} %collective-permute-done.1, bf16[1,512,512]{2,1,0:T(8,128)(2,1)} %collective-permute-done), kind=kLoop, calls=%fused_computation.1 | loop fusion | flops 1572864 | bytes 3145728 | tf_op jit(solution)/shard_map/concatenate | solution.py:132
  106.6 1.0 fusion.28
  107.6 1.0 fusion.30
  108.6 1.5 %add_convert_fusion = bf16[512,512]{1,0:T(8,128)(2,1)S(1)} fusion(f32[1536,512]{1,0:T(8,128)S(1)} %fusion.28, f32[1536,512]{1,0:T(8,128)S(1)} %fusion.30, bf16[1536,512]{1,0:T(8,128)(2,1)S(1)} %bitcast.116, f32[]{:T(128)S(6)} %sub.31, f32[]{:T(128)S(6)} %select_n.22, f32[]{:T(128)S(6)} %convert_element_type.146, f32[]{:T(128)S(6)} %convert_element_type.145, ...), kind=kOutput, calls=%fused_computation.37 | convolution fusion | flops 277348352 | bytes 6815800 | tf_op jit(solution)/shard_map/dot_general | solution.py:68
  110.1 0.7 pad_slice_fusion
  114.3 1.2 %fusion.3 = bf16[1,512,512]{2,1,0:T(8,128)(2,1)} fusion(f32[512,512]{1,0:T(8,128)S(1)} %convolution_add_fusion.1, bf16[512,512]{1,0:T(8,128)(2,1)S(1)} %bitcast.122, bf16[3,3,512,512]{3,2,1,0:T(8,128)(2,1)S(1)} %bitcast.121), kind=kOutput, calls=%fused_computation.24 | convolution fusion | flops 268959744 | bytes 2621440 | tf_op jit(solution)/shard_map/dot_general | solution.py:101
  (33 shorter events, 5.7 us)
Async XLA Ops:
  0.0 81.5 %copy-start = (bf16[512,512]{1,0:T(8,128)(2,1)S(1)}, bf16[512,512]{1,0:T(8,128)(2,1)}, u32[]{:S(2)}) copy-start(bf16[512,512]{1,0:T(8,128)(2,1)} %param.12) | copy-start | bytes 1572868
  0.0 11.2 %copy-start.3 = (bf16[512,512]{1,0:T(8,128)(2,1)S(1)}, bf16[512,512]{1,0:T(8,128)(2,1)}, u32[]{:S(2)}) copy-start(bf16[512,512]{1,0:T(8,128)(2,1)} %param.9) | copy-start | bytes 1572868
  1.3 28.5 %copy-start.4 = (bf16[512,512]{1,0:T(8,128)(2,1)S(1)}, bf16[512,512]{1,0:T(8,128)(2,1)}, u32[]{:S(2)}) copy-start(bf16[512,512]{1,0:T(8,128)(2,1)} %param.11) | copy-start | bytes 1572868
  4.9 20.1 %all-to-all-start.2 = ((bf16[1,32,16,512]{3,2,0,1:T(8,128)(2,1)}), bf16[1,32,16,512]{3,2,0,1:T(8,128)(2,1)S(1)}, u32[]{:S(2)}, u32[]{:S(2)}) async-start(bf16[1,32,16,512]{3,2,0,1:T(8,128)(2,1)} %fusion.7), calls=%async_computation.2 | async-start | bytes 1048576 | tf_op jit(solution)/shard_map/all_to_all | solution.py:118
  24.9 18.6 %all-to-all-start.1 = ((bf16[1,32,16,512]{3,2,0,1:T(8,128)(2,1)}), bf16[1,32,16,512]{3,2,0,1:T(8,128)(2,1)S(1)}, u32[]{:S(2)}, u32[]{:S(2)}) async-start(bf16[1,32,16,512]{3,2,0,1:T(8,128)(2,1)} %fusion.6), calls=%async_computation.1 | async-start | bytes 1048576 | tf_op jit(solution)/shard_map/all_to_all | solution.py:117
  31.1 50.4 %copy-start.1 = (bf16[1,512,512]{2,1,0:T(8,128)(2,1)S(1)}, bf16[1,512,512]{2,1,0:T(8,128)(2,1)}, u32[]{:S(2)}) copy-start(bf16[1,512,512]{2,1,0:T(8,128)(2,1)} %param.8) | copy-start | bytes 1572868
  43.6 18.6 %all-to-all-start = ((bf16[1,32,16,512]{3,2,0,1:T(8,128)(2,1)}), bf16[1,32,16,512]{3,2,0,1:T(8,128)(2,1)S(1)}, u32[]{:S(2)}, u32[]{:S(2)}) async-start(bf16[1,32,16,512]{3,2,0,1:T(8,128)(2,1)} %fusion.5), calls=%async_computation | async-start | bytes 1048576 | tf_op jit(solution)/shard_map/all_to_all | solution.py:119
  62.7 25.4 %copy-start.5 = (s32[4]{0:T(128)S(1)}, s32[4]{0:T(128)}, u32[]{:S(2)}) copy-start(s32[4]{0:T(128)} %param.15) | copy-start | bytes 52
  81.5 25.1 %copy-start.2 = (bf16[3,512,512]{2,1,0:T(8,128)(2,1)S(1)}, bf16[3,512,512]{2,1,0:T(8,128)(2,1)}, u32[]{:S(2)}) copy-start(bf16[3,512,512]{2,1,0:T(8,128)(2,1)} %param.13) | copy-start | bytes 4718596
  82.2 12.2 %collective-permute-start.1 = (bf16[1,512,512]{2,1,0:T(8,128)(2,1)S(1)}, bf16[1,512,512]{2,1,0:T(8,128)(2,1)}, u32[]{:S(2)}, u32[]{:S(2)}) collective-permute-start(bf16[1,512,512]{2,1,0:T(8,128)(2,1)S(1)} %fusion.14), channel_id=1, source_target_pairs={{0,1},{1,2},{2,3},{3,4},{4,5},{5,6},{6,7},{7,8},{8,9},{9,10},{10,1... | collective-permute-start | bytes 1572872 | tf_op jit(solution)/shard_map/ppermute | solution.py:17
  85.3 20.0 %collective-permute-start = (bf16[1,512,512]{2,1,0:T(8,128)(2,1)S(1)}, bf16[1,512,512]{2,1,0:T(8,128)(2,1)}, u32[]{:S(2)}, u32[]{:S(2)}) collective-permute-start(bf16[1,512,512]{2,1,0:T(8,128)(2,1)S(1)} %fusion.14), channel_id=1, source_target_pairs={{0,2},{1,3},{2,4},{3,5},{4,6},{5,7},{6,8},{7,9},{8,10},{9,11},{10,... | collective-permute-start | bytes 1572872 | tf_op jit(solution)/shard_map/ppermute | solution.py:17
  107.6 3.2 %slice-start = ((s8[4718592]{0:T(1024)(128)(4,1)}), s8[4194304]{0:T(1024)(128)(4,1)S(1)}, s32[]{:S(2)}) async-start(s8[4718592]{0:T(1024)(128)(4,1)} %bitcast.120), calls=%async_computation.4 | async-start | bytes 8388608
  108.6 2.2 %slice-start.1 = ((s8[4718592]{0:T(1024)(128)(4,1)}), s8[524288]{0:T(1024)(128)(4,1)S(1)}, s32[]{:S(2)}) async-start(s8[4718592]{0:T(1024)(128)(4,1)} %bitcast.120), calls=%async_computation.5 | async-start | bytes 1048576
where the time goes:
time: 118 us; the launch traced here: 116 us
  waiting for transfers between devices  51.3 us (43%)
  starting transfers between devices  22 us (19%)
  blocking collectives  18.4 us (16%)
  matrix products  14.7 us (12%)
  other arithmetic  6.02 us (5%)
  between operations  2.18 us (2%)
    all_to_all x1, blocking collectives, body(): lax.all_to_all(attended, 'tm', split_axis=0, concat_axis=1, tiled=True)  18.4 us
    ppermute x2, waiting for transfers between devices, passed_along(): return lax.ppermute(block, axis, route)  13.2 us
    all_to_all x1, waiting for transfers between devices, body(): lax.all_to_all(values, 'tm', split_axis=1, concat_axis=0, tiled=True)  13 us
    all_to_all x1, waiting for transfers between devices, body(): lax.all_to_all(key_rows, 'tm', split_axis=1, concat_axis=0, tiled=True)  12.5 us
    all_to_all x1, waiting for transfers between devices, body(): lax.all_to_all(queries, 'tm', split_axis=1, concat_axis=0, tiled=True)  12.5 us
    all_to_all x1, starting transfers between devices, body(): lax.all_to_all(key_rows, 'tm', split_axis=1, concat_axis=0, tiled=True)  6.3 us
    ppermute x2, starting transfers between devices, passed_along(): return lax.ppermute(block, axis, route)  5.93 us
    dot_general x4, matrix products, project(): jnp.dot(array.reshape(-1, extent[-1]), weight, preferred_element_type=jnp...  5.27 us
  transfers between devices with their start and end apart: 5, of which 5 were waited for; matrix products, arithmetic and copies ran while one was open for 4% of the time, Pallas kernels for 0%

commit v1 on v0

--- a/solution.py
+++ b/solution.py
@@ -1,6 +1,10 @@
+import functools
+
 import jax
 import jax.numpy as jnp
 from jax import lax
+from jax.experimental import pallas as pl
+from jax.experimental.pallas import tpu as pltpu
 from jax.sharding import PartitionSpec as P
 
 PH = 16
@@ -133,8 +137,385 @@
     return space_mix(blended, hidden, w_space)
 
 
+BS = 4
+BLOCK = BS * BS
+GROUP = 128
+
+
+def iota(shape, dim):
+    return lax.broadcasted_iota(jnp.int32, shape, dim)
+
+
+def one_hot(target, columns):
+    rows = target.shape[0]
+    return (jnp.broadcast_to(target, (rows, columns)) == iota((rows, columns), 1)).astype(
+        jnp.float32
+    ).astype(jnp.bfloat16)
+
+
+def matmul(left, right):
+    return jnp.dot(left, right, preferred_element_type=jnp.float32)
+
+
+def place_of(device):
+    core, x, y, z = device % 2, (device // 2) % 2, (device // 4) % 2, device // 8
+    return 2 * y + (x + y) % 2, 2 * z + core
+
+
+def device_at(row, column):
+    y = row // 2
+    return (column // 2) * 8 + y * 4 + ((row % 2 + y) % 2) * 2 + column % 2
+
+
+def window_position():
+    r = iota((PH * PW, 1), 0)
+    device, q = r >> 4, r & 15
+    core, x, y, z = device & 1, (device >> 1) & 1, (device >> 2) & 1, device >> 3
+    row, column = 2 * y + (x ^ y), 2 * z + core
+    return (row * BS + (q >> 2)) * PW + column * BS + (q & 3)
+
+
+def block_position():
+    p = iota((PH * PW, 1), 0)
+    py, px = p >> 5, p & 31
+    row, column = py >> 2, px >> 2
+    y = row >> 1
+    device = (column >> 1) * 8 + y * 4 + ((row & 1) ^ y) * 2 + (column & 1)
+    return device * BLOCK + (py & 3) * BS + (px & 3)
+
+
+def normalized(wide):
+    scale = lax.rsqrt(jnp.mean(wide * wide, axis=-1, keepdims=True) + epsilon)
+    return (wide * scale).astype(jnp.bfloat16)
+
+
+def silu(v):
+    return v / (1.0 + jnp.exp(-v))
+
+
+def block_kernel(
+    starts,
+    latents,
+    wq_any,
+    wk_any,
+    wv_any,
+    wo_any,
+    wt_any,
+    ws_any,
+    out,
+    wq,
+    wk,
+    wv,
+    wo,
+    wt,
+    ws,
+    outgoing,
+    arrived,
+    ext,
+    back,
+    returned,
+    current,
+    weight_sem,
+    sent,
+    got,
+    halo_sent,
+    halo_got,
+    back_sent,
+    back_got,
+    *,
+    n,
+):
+    frames = n
+    channels = latents.shape[-1]
+    rows = BLOCK * frames
+    me = lax.axis_index("tm")
+    mesh_id = pl.DeviceIdType.MESH
+
+    barrier = pltpu.get_barrier_semaphore()
+
+    @pl.loop(1, n)
+    def _(k):
+        pl.semaphore_signal(
+            barrier, inc=1, device_id={"tm": (me + k) % n}, device_id_type=mesh_id
+        )
+
+    weights = [
+        pltpu.make_async_copy(source, target, weight_sem.at[i])
+        for i, (source, target) in enumerate(
+            ((wq_any, wq), (wk_any, wk), (wv_any, wv), (wo_any, wo), (wt_any, wt), (ws_any, ws))
+        )
+    ]
+    for copy in weights:
+        copy.start()
+
+    outgoing[...] = (
+        matmul(one_hot(window_position(), PH * PW), latents[0])
+        .astype(jnp.bfloat16)
+        .reshape(n, BLOCK, channels)
+    )
+    pl.semaphore_wait(barrier, n - 1)
+
+    def in_copy(k):
+        peer = (me + k) % n
+        return pltpu.make_async_remote_copy(
+            src_ref=outgoing.at[peer],
+            dst_ref=arrived.at[me],
+            send_sem=sent.at[k],
+            recv_sem=got.at[k],
+            device_id={"tm": peer},
+            device_id_type=mesh_id,
+        )
+
+    @pl.loop(1, n)
+    def _(k):
+        in_copy(k).start()
+
+    arrived[me] = outgoing[me]
+
+    row, column = place_of(me)
+    edge = jnp.zeros((BS + 2, frames, channels), jnp.bfloat16)
+
+    @pl.when(row == 0)
+    def _():
+        ext[0] = edge
+
+    @pl.when(row == PH // BS - 1)
+    def _():
+        ext[BS + 1] = edge
+
+    @pl.when(column == 0)
+    def _():
+        for i in range(BS + 2):
+            ext[i, 0] = edge[0]
+
+    @pl.when(column == PW // BS - 1)
+    def _():
+        for i in range(BS + 2):
+            ext[i, BS + 1] = edge[0]
+
+    r = iota((GROUP, 1), 0)
+    frame = r % frames
+    base = r - frame
+    new_start = jnp.zeros((GROUP, 1), jnp.int32)
+    for t in range(starts.shape[0]):
+        new_start = jnp.maximum(new_start, jnp.where(frame >= starts[t], starts[t], 0))
+    old_start = jnp.zeros((GROUP, 1), jnp.int32)
+    for t in range(starts.shape[0]):
+        old_start = jnp.maximum(old_start, jnp.where(new_start > starts[t], starts[t], 0))
+    inside = frame - new_start
+    fade = jnp.where(
+        jnp.logical_and(new_start > 0, inside < OV),
+        (inside + 1).astype(jnp.float32) / float(OV + 1),
+        jnp.float32(1.0),
+    )
+    lags = [
+        [one_hot(base + jnp.maximum(frame - j, start), GROUP) for j in (1, 2)]
+        for start in (new_start, old_start)
+    ]
+    other = iota((GROUP, GROUP), 1)
+    wide_frame, wide_base = jnp.broadcast_to(frame, other.shape), jnp.broadcast_to(base, other.shape)
+    seen = jnp.logical_and(other >= wide_base, other <= wide_base + wide_frame)
+
+    flat = iota((rows, 1), 0)
+    by_position = one_hot((flat % frames) * BLOCK + flat // frames, rows)
+    by_frame = one_hot((flat % BLOCK) * frames + flat // BLOCK, rows)
+
+    @pl.loop(1, n)
+    def _(k):
+        in_copy(k).wait_recv()
+
+    held = matmul(by_position, arrived[...].reshape(rows, channels))
+    normed = normalized(held)
+    for copy in weights[:3]:
+        copy.wait()
+    queries = matmul(normed, wq[...]).astype(jnp.bfloat16)
+    key_rows = matmul(normed, wk[...]).astype(jnp.bfloat16)
+    values = matmul(normed, wv[...]).astype(jnp.bfloat16)
+    attended = []
+    for g in range(rows // GROUP):
+        part = slice(g * GROUP, (g + 1) * GROUP)
+        scores = lax.dot_general(
+            queries[part],
+            key_rows[part],
+            (((1,), (1,)), ((), ())),
+            preferred_element_type=jnp.float32,
+        ) * (channels ** (-0.5))
+        scores = jnp.where(seen, scores, jnp.float32(-1e30))
+        expo = jnp.exp(scores - jnp.max(scores, axis=-1, keepdims=True))
+        share = (expo / jnp.sum(expo, axis=-1, keepdims=True)).astype(jnp.bfloat16)
+        attended.append(matmul(share, values[part]).astype(jnp.bfloat16))
+    weights[3].wait()
+    hidden = (held + matmul(jnp.concatenate(attended, axis=0), wo[...])).astype(jnp.bfloat16)
+    smooth = normalized(hidden.astype(jnp.float32))
+
+    weights[4].wait()
+    current[...] = matmul(smooth, wt[0])
+    lag_weights = wt[1:3].reshape(2 * channels, channels)
+    mixes = []
+    for pair in lags:
+        lagged = jnp.concatenate(
+            [
+                jnp.concatenate(
+                    [
+                        matmul(lag, smooth[g * GROUP : (g + 1) * GROUP]).astype(jnp.bfloat16)
+                        for lag in pair
+                    ],
+                    axis=1,
+                )
+                for g in range(rows // GROUP)
+            ],
+            axis=0,
+        )
+        mixes.append(current[...] + matmul(lagged, lag_weights))
+    fade = jnp.concatenate([fade] * (rows // GROUP), axis=0)
+    blended = (fade * silu(mixes[0]) + (1.0 - fade) * silu(mixes[1])).astype(jnp.bfloat16)
+    ext[1 : BS + 1, 1 : BS + 1] = blended.reshape(BS, BS, frames, channels)
+
+    def span(step, sending):
+        if step == 0:
+            return pl.ds(1, BS)
+        if sending:
+            return pl.ds(1 if step < 0 else BS, 1)
+        return pl.ds(BS + 1 if step < 0 else 0, 1)
+
+    halo = []
+    for i, (down, right) in enumerate(
+        ((-1, 0), (1, 0), (0, -1), (0, 1), (-1, -1), (-1, 1), (1, -1), (1, 1))
+    ):
+        to_row, to_column = row + down, column + right
+        there = jnp.logical_and(
+            jnp.logical_and(to_row >= 0, to_row < PH // BS),
+            jnp.logical_and(to_column >= 0, to_column < PW // BS),
+        )
+        from_row, from_column = row - down, column - right
+        comes = jnp.logical_and(
+            jnp.logical_and(from_row >= 0, from_row < PH // BS),
+            jnp.logical_and(from_column >= 0, from_column < PW // BS),
+        )
+        peer = device_at((to_row + PH // BS) % (PH // BS), (to_column + PW // BS) % (PW // BS))
+        copy = pltpu.make_async_remote_copy(
+            src_ref=ext.at[span(down, True), span(right, True)],
+            dst_ref=ext.at[span(down, False), span(right, False)],
+            send_sem=halo_sent.at[i],
+            recv_sem=halo_got.at[i],
+            device_id={"tm": peer},
+            device_id_type=mesh_id,
+        )
+        halo.append((copy, there, comes))
+
+    for copy, there, comes in halo:
+
+        @pl.when(there)
+        def _():
+            copy.start()
+
+    weights[5].wait()
+    total = hidden.astype(jnp.float32) + matmul(blended, ws[1, 1])
+
+    for copy, there, comes in halo:
+
+        @pl.when(comes)
+        def _():
+            copy.wait_recv()
+
+    for a in range(3):
+        for b in range(3):
+            if (a, b) != (1, 1):
+                window = ext[a : a + BS, b : b + BS].reshape(rows, channels)
+                total = total + matmul(window, ws[a, b])
+    decoded = total.astype(jnp.bfloat16)
+    back[...] = (
+        matmul(by_frame, decoded).astype(jnp.bfloat16).reshape(frames, BLOCK, channels)
+    )
+
+    def back_copy(k):
+        peer = (me + k) % n
+        return pltpu.make_async_remote_copy(
+            src_ref=back.at[peer],
+            dst_ref=returned.at[me],
+            send_sem=back_sent.at[k],
+            recv_sem=back_got.at[k],
+            device_id={"tm": peer},
+            device_id_type=mesh_id,
+        )
+
+    @pl.loop(1, n)
+    def _(k):
+        back_copy(k).start()
+
+    returned[me] = back[me]
+    to_window = one_hot(block_position(), PH * PW)
+
+    @pl.loop(1, n)
+    def _(k):
+        in_copy(k).wait_send()
+
+    for copy, there, comes in halo:
+
+        @pl.when(there)
+        def _():
+            copy.wait_send()
+
+    @pl.loop(1, n)
+    def _(k):
+        back_copy(k).wait_recv()
+
+    out[0] = matmul(to_window, returned[...].reshape(PH * PW, channels)).astype(jnp.bfloat16)
+
+    @pl.loop(1, n)
+    def _(k):
+        back_copy(k).wait_send()
+
+
+def block_body(latents, w_query, w_key, w_value, w_out, w_time, w_space, tile_starts):
+    n = lax.axis_size("tm")
+    channels = latents.shape[-1]
+    vmem = pl.BlockSpec(memory_space=pltpu.VMEM)
+    anywhere = pl.BlockSpec(memory_space=pl.ANY)
+    dma = pltpu.SemaphoreType.DMA
+    bf16 = jnp.bfloat16
+    return pl.pallas_call(
+        functools.partial(block_kernel, n=n),
+        out_shape=jax.ShapeDtypeStruct(latents.shape, bf16),
+        in_specs=[pl.BlockSpec(memory_space=pltpu.SMEM), vmem] + [anywhere] * 6,
+        out_specs=vmem,
+        scratch_shapes=[
+            pltpu.VMEM(w_query.shape, bf16),
+            pltpu.VMEM(w_key.shape, bf16),
+            pltpu.VMEM(w_value.shape, bf16),
+            pltpu.VMEM(w_out.shape, bf16),
+            pltpu.VMEM(w_time.shape, bf16),
+            pltpu.VMEM(w_space.shape, bf16),
+            pltpu.VMEM((n, BLOCK, channels), bf16),
+            pltpu.VMEM((n, BLOCK, channels), bf16),
+            pltpu.VMEM((BS + 2, BS + 2, n, channels), bf16),
+            pltpu.VMEM((n, BLOCK, channels), bf16),
+            pltpu.VMEM((n, BLOCK, channels), bf16),
+            pltpu.VMEM((n * BLOCK, channels), jnp.float32),
+            dma((6,)),
+            dma((n,)),
+            dma((n,)),
+            dma((8,)),
+            dma((8,)),
+            dma((n,)),
+            dma((n,)),
+        ],
+        compiler_params=pltpu.CompilerParams(
+            collective_id=0, has_side_effects=True, vmem_limit_bytes=48 * 2**20
+        ),
+    )(tile_starts, latents, w_query, w_key, w_value, w_out, w_time, w_space)
+
+
+def any_body(latents, *rest):
+    frames_dev, row_count, channels = latents.shape
+    blocks = (PH // BS) * (PW // BS)
+    if frames_dev == 1 and lax.axis_size("tm") == blocks and row_count == PH * PW:
+        return block_body(latents, *rest)
+    return body(latents, *rest)
+
+
 def solution(mesh):
     placed = (P(("groups", "tm"), None, None), P(), P(), P(), P(), P(), P(), P("groups"))
     return jax.shard_map(
-        body, mesh=mesh, in_specs=placed, out_specs=P(("groups", "tm"), None, None), check_vma=False
-    )
+        any_body, mesh=mesh, in_specs=placed, out_specs=P(("groups", "tm"), None, None), check_vma=False
+    )

time: 118 us -> 55.4 us (0.47); the launches traced: 116 us -> 55 us
  waiting for transfers between devices: 51.3 us -> 0 us
  Pallas kernels: 0 us -> 46.9 us
  starting transfers between devices: 22 us -> 0 us
  blocking collectives: 18.4 us -> 0 us
  matrix products: 14.7 us -> 0 us
  local copies, waits for them, and re-layouts: 0.99 us -> 8.06 us
  other arithmetic: 6.02 us -> 0 us
  between operations: 2.18 us -> 0.02 us
    pallas_call x0 -> x1, Pallas kernels: none -> 46.9 us  [block_body(): pl.pallas_call(functools.partial(block_kernel, n=n), out_shape=jax.ShapeD...]
    all_to_all x3 -> x0, waiting for transfers between devices: 38.1 us -> none  [the longest x1 13 us: body(): lax.all_to_all(values, 'tm', split_axis=1, concat_axis=0, tiled=True)]
    all_to_all x1 -> x0, blocking collectives: 18.4 us -> none  [body(): lax.all_to_all(attended, 'tm', split_axis=0, concat_axis=1, tiled=True)]
    all_to_all x3 -> x0, starting transfers between devices: 16 us -> none  [the longest x1 6.3 us: body(): lax.all_to_all(key_rows, 'tm', split_axis=1, concat_axis=0, tiled=True)]
    dot_general x17 -> x0, matrix products: 14 us -> none  [the longest x4 5.27 us: project(): jnp.dot(array.reshape(-1, extent[-1]), weight, preferred_element_type=jnp...]
    ppermute x2 -> x0, waiting for transfers between devices: 13.2 us -> none  [passed_along(): return lax.ppermute(block, axis, route)]
    unnamed x16 -> x15, local copies, waits for them, and re-layouts: 0.04 us -> 8.06 us
    ppermute x2 -> x0, starting transfers between devices: 5.93 us -> none  [passed_along(): return lax.ppermute(block, axis, route)]
  transfers between devices with their start and end apart: 5 -> 0, of which waited for: 5 -> 0; matrix products, arithmetic and copies ran while one was open for 4% -> 0% of each run, Pallas kernels for 0% -> 0%
where the time goes in v1:
time: 55.4 us; the launch traced here: 55 us
  Pallas kernels  46.9 us (85%)
  local copies, waits for them, and re-layouts  8.06 us (15%)
    pallas_call x1, Pallas kernels, block_body(): pl.pallas_call(functools.partial(block_kernel, n=n), out_shape=jax.ShapeD...  46.9 us
    unnamed x15, local copies, waits for them, and re-layouts  8.06 us

profile of v1, /device:TPU:13, one launch (start us, length us, event | category | flops | bytes accessed | tf_op | source)
XLA Modules:
  0.0 55.0 jit_solution(10872535957246594085)
XLA Ops:
  0.0 0.0 copy-start
  0.0 1.4 %copy-done = bf16[3,512,512]{2,1,0:T(8,128)(2,1)S(1)} copy-done((bf16[3,512,512]{2,1,0:T(8,128)(2,1)S(1)}, bf16[3,512,512]{2,1,0:T(8,128)(2,1)}, u32[]{:S(2)}) %copy-start) | copy-done | bytes 1572888
  1.4 0.0 copy-start.1
  1.4 1.0 %copy-done.1 = bf16[1,512,512]{2,1,0:T(8,128)(2,1)S(1)} copy-done((bf16[1,512,512]{2,1,0:T(8,128)(2,1)S(1)}, bf16[1,512,512]{2,1,0:T(8,128)(2,1)}, u32[]{:S(2)}) %copy-start.1) | copy-done | bytes 524312
  2.5 0.0 copy-start.2
  2.5 1.0 %copy-done.2 = bf16[512,512]{1,0:T(8,128)(2,1)S(1)} copy-done((bf16[512,512]{1,0:T(8,128)(2,1)S(1)}, bf16[512,512]{1,0:T(8,128)(2,1)}, u32[]{:S(2)}) %copy-start.2) | copy-done | bytes 524312
  3.5 0.0 copy-start.3
  3.5 1.0 %copy-done.3 = bf16[512,512]{1,0:T(8,128)(2,1)S(1)} copy-done((bf16[512,512]{1,0:T(8,128)(2,1)S(1)}, bf16[512,512]{1,0:T(8,128)(2,1)}, u32[]{:S(2)}) %copy-start.3) | copy-done | bytes 524312
  4.5 0.0 copy-start.4
  4.5 1.0 %copy-done.4 = bf16[512,512]{1,0:T(8,128)(2,1)S(1)} copy-done((bf16[512,512]{1,0:T(8,128)(2,1)S(1)}, bf16[512,512]{1,0:T(8,128)(2,1)}, u32[]{:S(2)}) %copy-start.4) | copy-done | bytes 524312
  5.6 0.0 copy-start.5
  5.6 1.0 %copy-done.5 = bf16[512,512]{1,0:T(8,128)(2,1)S(1)} copy-done((bf16[512,512]{1,0:T(8,128)(2,1)S(1)}, bf16[512,512]{1,0:T(8,128)(2,1)}, u32[]{:S(2)}) %copy-start.5) | copy-done | bytes 524312
  6.6 0.0 copy-start.6
  6.6 0.7 %copy-done.6 = s32[4]{0:T(128)S(1)} copy-done((s32[4]{0:T(128)S(1)}, s32[4]{0:T(128)}, u32[]{:S(2)}) %copy-start.6) | copy-done | bytes 40
  7.3 46.9 %shard_map.82 = bf16[1,512,512]{2,1,0:T(8,128)(2,1)S(1)} custom-call(s32[4]{0:T(128)S(1)} %copy-done.6, bf16[1,512,512]{2,1,0:T(8,128)(2,1)S(1)} %copy-done.1, bf16[512,512]{1,0:T(8,128)(2,1)S(1)} %copy-done.2, bf16[512,512]{1,0:T(8,128)(2,1)S(1)} %copy-done.3, bf16[512,512]{1,0:T(8,128)(2,1)S(1)} %copy-done.4, bf16[512,512]{1,0:T(8,128)(2,1)S(1)} %copy-done.5, ...), custom_call_target="tpu_custom_call" | custom-call | tf_op jit(solution)/shard_map/pallas_call | solution.py:477
  54.2 0.8 %copy.10 = bf16[1,512,512]{2,1,0:T(8,128)(2,1)} copy(bf16[1,512,512]{2,1,0:T(8,128)(2,1)S(1)} %shard_map.82) | data formatting | bytes 1048576
Async XLA Ops:
  0.0 1.4 %copy-start = (bf16[3,512,512]{2,1,0:T(8,128)(2,1)S(1)}, bf16[3,512,512]{2,1,0:T(8,128)(2,1)}, u32[]{:S(2)}) copy-start(bf16[3,512,512]{2,1,0:T(8,128)(2,1)} %wt_any.1) | copy-start | bytes 4718596
  1.4 1.0 %copy-start.1 = (bf16[1,512,512]{2,1,0:T(8,128)(2,1)S(1)}, bf16[1,512,512]{2,1,0:T(8,128)(2,1)}, u32[]{:S(2)}) copy-start(bf16[1,512,512]{2,1,0:T(8,128)(2,1)} %latents.1) | copy-start | bytes 1572868
  2.5 1.0 %copy-start.2 = (bf16[512,512]{1,0:T(8,128)(2,1)S(1)}, bf16[512,512]{1,0:T(8,128)(2,1)}, u32[]{:S(2)}) copy-start(bf16[512,512]{1,0:T(8,128)(2,1)} %wq_any.1) | copy-start | bytes 1572868
  3.5 1.0 %copy-start.3 = (bf16[512,512]{1,0:T(8,128)(2,1)S(1)}, bf16[512,512]{1,0:T(8,128)(2,1)}, u32[]{:S(2)}) copy-start(bf16[512,512]{1,0:T(8,128)(2,1)} %wk_any.1) | copy-start | bytes 1572868
  4.5 1.0 %copy-start.4 = (bf16[512,512]{1,0:T(8,128)(2,1)S(1)}, bf16[512,512]{1,0:T(8,128)(2,1)}, u32[]{:S(2)}) copy-start(bf16[512,512]{1,0:T(8,128)(2,1)} %wv_any.1) | copy-start | bytes 1572868
  5.6 1.0 %copy-start.5 = (bf16[512,512]{1,0:T(8,128)(2,1)S(1)}, bf16[512,512]{1,0:T(8,128)(2,1)}, u32[]{:S(2)}) copy-start(bf16[512,512]{1,0:T(8,128)(2,1)} %wo_any.1) | copy-start | bytes 1572868
  6.6 0.7 %copy-start.6 = (s32[4]{0:T(128)S(1)}, s32[4]{0:T(128)}, u32[]{:S(2)}) copy-start(s32[4]{0:T(128)} %starts.1) | copy-start | bytes 52

commit v2 on v1

--- a/solution.py
+++ b/solution.py
@@ -410,7 +410,7 @@
             copy.start()
 
     weights[5].wait()
-    total = hidden.astype(jnp.float32) + matmul(blended, ws[1, 1])
+    current[...] = hidden.astype(jnp.float32) + matmul(blended, ws[1, 1])
 
     for copy, there, comes in halo:
 
@@ -418,32 +418,39 @@
         def _():
             copy.wait_recv()
 
-    for a in range(3):
-        for b in range(3):
-            if (a, b) != (1, 1):
-                window = ext[a : a + BS, b : b + BS].reshape(rows, channels)
-                total = total + matmul(window, ws[a, b])
-    decoded = total.astype(jnp.bfloat16)
-    back[...] = (
-        matmul(by_frame, decoded).astype(jnp.bfloat16).reshape(frames, BLOCK, channels)
-    )
-
-    def back_copy(k):
+    half = channels // 2
+
+    def back_copy(k, h):
         peer = (me + k) % n
         return pltpu.make_async_remote_copy(
-            src_ref=back.at[peer],
-            dst_ref=returned.at[me],
-            send_sem=back_sent.at[k],
-            recv_sem=back_got.at[k],
+            src_ref=back.at[h, peer],
+            dst_ref=returned.at[h, me],
+            send_sem=back_sent.at[h, k],
+            recv_sem=back_got.at[h, k],
             device_id={"tm": peer},
             device_id_type=mesh_id,
         )
 
-    @pl.loop(1, n)
-    def _(k):
-        back_copy(k).start()
-
-    returned[me] = back[me]
+    for h in range(2):
+        part = slice(h * half, (h + 1) * half)
+        total = current[:, part]
+        for a in range(3):
+            for b in range(3):
+                if (a, b) != (1, 1):
+                    window = ext[a : a + BS, b : b + BS].reshape(rows, channels)
+                    total = total + matmul(window, ws[a, b, :, part])
+        back[h] = (
+            matmul(by_frame, total.astype(jnp.bfloat16))
+            .astype(jnp.bfloat16)
+            .reshape(frames, BLOCK, half)
+        )
+
+        @pl.loop(1, n)
+        def _(k):
+            back_copy(k, h).start()
+
+        returned[h, me] = back[h, me]
+
     to_window = one_hot(block_position(), PH * PW)
 
     @pl.loop(1, n)
@@ -456,22 +463,28 @@
         def _():
             copy.wait_send()
 
-    @pl.loop(1, n)
-    def _(k):
-        back_copy(k).wait_recv()
-
-    out[0] = matmul(to_window, returned[...].reshape(PH * PW, channels)).astype(jnp.bfloat16)
-
-    @pl.loop(1, n)
-    def _(k):
-        back_copy(k).wait_send()
+    for h in range(2):
+
+        @pl.loop(1, n)
+        def _(k):
+            back_copy(k, h).wait_recv()
+
+        out[0, :, h * half : (h + 1) * half] = matmul(
+            to_window, returned[h].reshape(PH * PW, half)
+        ).astype(jnp.bfloat16)
+
+    for h in range(2):
+
+        @pl.loop(1, n)
+        def _(k):
+            back_copy(k, h).wait_send()
 
 
 def block_body(latents, w_query, w_key, w_value, w_out, w_time, w_space, tile_starts):
     n = lax.axis_size("tm")
     channels = latents.shape[-1]
     vmem = pl.BlockSpec(memory_space=pltpu.VMEM)
-    anywhere = pl.BlockSpec(memory_space=pl.ANY)
+    anywhere = pl.BlockSpec(memory_space=pltpu.HBM)
     dma = pltpu.SemaphoreType.DMA
     bf16 = jnp.bfloat16
     return pl.pallas_call(
@@ -489,19 +502,19 @@
             pltpu.VMEM((n, BLOCK, channels), bf16),
             pltpu.VMEM((n, BLOCK, channels), bf16),
             pltpu.VMEM((BS + 2, BS + 2, n, channels), bf16),
-            pltpu.VMEM((n, BLOCK, channels), bf16),
-            pltpu.VMEM((n, BLOCK, channels), bf16),
+            pltpu.VMEM((2, n, BLOCK, channels // 2), bf16),
+            pltpu.VMEM((2, n, BLOCK, channels // 2), bf16),
             pltpu.VMEM((n * BLOCK, channels), jnp.float32),
             dma((6,)),
             dma((n,)),
             dma((n,)),
             dma((8,)),
             dma((8,)),
-            dma((n,)),
-            dma((n,)),
+            dma((2, n)),
+            dma((2, n)),
         ],
         compiler_params=pltpu.CompilerParams(
-            collective_id=0, has_side_effects=True, vmem_limit_bytes=48 * 2**20
+            collective_id=0, has_side_effects=True, vmem_limit_bytes=60 * 2**20
         ),
     )(tile_starts, latents, w_query, w_key, w_value, w_out, w_time, w_space)
 

time: 55.4 us -> 51.9 us (0.937)
  local copies, waits for them, and re-layouts: 8.06 us -> 1.87 us
  Pallas kernels: 46.9 us -> 49.2 us
    unnamed x15 -> x1, local copies, waits for them, and re-layouts: 8.06 us -> 1.87 us
    pallas_call x1, Pallas kernels: 46.9 us -> 49.2 us  [block_body(): pl.pallas_call(functools.partial(block_kernel, n=n), out_shape=jax.ShapeD...]
where the time goes in v2:
time: 51.9 us; the launch traced here: 51.1 us
  Pallas kernels  49.2 us (95%)
  local copies, waits for them, and re-layouts  1.87 us (4%)
    pallas_call x1, Pallas kernels, block_body(): pl.pallas_call(functools.partial(block_kernel, n=n), out_shape=jax.ShapeD...  49.2 us
    unnamed x1, local copies, waits for them, and re-layouts  1.87 us

profile of v2, /device:TPU:13, one launch (start us, length us, event | category | flops | bytes accessed | tf_op | source)
XLA Modules:
  0.0 51.1 jit_solution(6174040267214989331)
XLA Ops:
  0.0 49.2 %shard_map.82 = bf16[1,512,512]{2,1,0:T(8,128)(2,1)} custom-call(s32[4]{0:T(128)} %starts.1, bf16[1,512,512]{2,1,0:T(8,128)(2,1)} %latents.1, bf16[512,512]{1,0:T(8,128)(2,1)} %wq_any.1, bf16[512,512]{1,0:T(8,128)(2,1)} %wk_any.1, bf16[512,512]{1,0:T(8,128)(2,1)} %wv_any.1, bf16[512,512]{1,0:T(8,128)(2,1)} %wo_any.1, bf16[3,512,512]{2,1,0:T(8,128)(2,1)} %wt_any.1, ...), custom_call_target="tpu_custom_call" | custom-call | tf_op jit(solution)/shard_map/pallas_call | solution.py:490
  49.3 1.9 %copy.10 = bf16[1,512,512]{2,1,0:T(8,128)(2,1)} copy(bf16[1,512,512]{2,1,0:T(8,128)(2,1)} %shard_map.82) | data formatting | bytes 1048576

commit v3 on v2

--- a/solution.py
+++ b/solution.py
@@ -412,11 +412,20 @@
     weights[5].wait()
     current[...] = hidden.astype(jnp.float32) + matmul(blended, ws[1, 1])
 
-    for copy, there, comes in halo:
-
-        @pl.when(comes)
-        def _():
-            copy.wait_recv()
+    def arrive(chosen):
+        for copy, there, comes in chosen:
+
+            @pl.when(comes)
+            def _():
+                copy.wait_recv()
+
+    arrive(halo[2:4])
+    total = current[...]
+    for b in (0, 2):
+        window = ext[1 : BS + 1, b : b + BS].reshape(rows, channels)
+        total = total + matmul(window, ws[1, b])
+    current[...] = total
+    arrive(halo[:2] + halo[4:])
 
     half = channels // 2
 
@@ -436,7 +445,7 @@
         total = current[:, part]
         for a in range(3):
             for b in range(3):
-                if (a, b) != (1, 1):
+                if a != 1:
                     window = ext[a : a + BS, b : b + BS].reshape(rows, channels)
                     total = total + matmul(window, ws[a, b, :, part])
         back[h] = (

time: 51.9 us -> 51.4 us (level)
    pallas_call x1, Pallas kernels: 49.2 us -> 48.7 us  [block_body(): pl.pallas_call(functools.partial(block_kernel, n=n), out_shape=jax.ShapeD...]
where the time goes in v3:
time: 51.4 us; the launch traced here: 50.6 us
  Pallas kernels  48.7 us (95%)
  local copies, waits for them, and re-layouts  1.87 us (4%)
    pallas_call x1, Pallas kernels, block_body(): pl.pallas_call(functools.partial(block_kernel, n=n), out_shape=jax.ShapeD...  48.7 us
    unnamed x1, local copies, waits for them, and re-layouts  1.87 us

profile of v3, /device:TPU:13, one launch (start us, length us, event | category | flops | bytes accessed | tf_op | source)
XLA Modules:
  0.0 50.6 jit_solution(8049773746887386561)
XLA Ops:
  0.0 48.7 %shard_map.82 = bf16[1,512,512]{2,1,0:T(8,128)(2,1)} custom-call(s32[4]{0:T(128)} %starts.1, bf16[1,512,512]{2,1,0:T(8,128)(2,1)} %latents.1, bf16[512,512]{1,0:T(8,128)(2,1)} %wq_any.1, bf16[512,512]{1,0:T(8,128)(2,1)} %wk_any.1, bf16[512,512]{1,0:T(8,128)(2,1)} %wv_any.1, bf16[512,512]{1,0:T(8,128)(2,1)} %wo_any.1, bf16[3,512,512]{2,1,0:T(8,128)(2,1)} %wt_any.1, ...), custom_call_target="tpu_custom_call" | custom-call | tf_op jit(solution)/shard_map/pallas_call | solution.py:499
  48.7 1.9 %copy.10 = bf16[1,512,512]{2,1,0:T(8,128)(2,1)} copy(bf16[1,512,512]{2,1,0:T(8,128)(2,1)} %shard_map.82) | data formatting | bytes 1048576

commit v4 on v3

--- a/solution.py
+++ b/solution.py
@@ -268,7 +268,7 @@
 
     @pl.loop(1, n)
     def _(k):
-        in_copy(k).start()
+        in_copy(k % 2 * ((k + 1) // 2) + (1 - k % 2) * (n - k // 2)).start()
 
     arrived[me] = outgoing[me]
 
@@ -456,7 +456,7 @@
 
         @pl.loop(1, n)
         def _(k):
-            back_copy(k, h).start()
+            back_copy(k % 2 * ((k + 1) // 2) + (1 - k % 2) * (n - k // 2), h).start()
 
         returned[h, me] = back[h, me]
 

time: 51.4 us -> 53.5 us (1.041)
  the two profiles are of different devices: /device:TPU:13 before, /device:TPU:0 now
where the time goes in v4:
time: 53.5 us; the launch traced here: 53.3 us
  Pallas kernels  51.4 us (96%)
  local copies, waits for them, and re-layouts  1.87 us (3%)
    pallas_call x1, Pallas kernels, block_body(): pl.pallas_call(functools.partial(block_kernel, n=n), out_shape=jax.ShapeD...  51.4 us
    unnamed x1, local copies, waits for them, and re-layouts  1.87 us

profile of v4, /device:TPU:0, one launch (start us, length us, event | category | flops | bytes accessed | tf_op | source)
XLA Modules:
  0.0 53.3 jit_solution(6336811027016729218)
XLA Ops:
  0.0 51.4 %shard_map.82 = bf16[1,512,512]{2,1,0:T(8,128)(2,1)} custom-call(s32[4]{0:T(128)} %starts.1, bf16[1,512,512]{2,1,0:T(8,128)(2,1)} %latents.1, bf16[512,512]{1,0:T(8,128)(2,1)} %wq_any.1, bf16[512,512]{1,0:T(8,128)(2,1)} %wk_any.1, bf16[512,512]{1,0:T(8,128)(2,1)} %wv_any.1, bf16[512,512]{1,0:T(8,128)(2,1)} %wo_any.1, bf16[3,512,512]{2,1,0:T(8,128)(2,1)} %wt_any.1, ...), custom_call_target="tpu_custom_call" | custom-call | tf_op jit(solution)/shard_map/pallas_call | solution.py:499
  51.4 1.9 %copy.10 = bf16[1,512,512]{2,1,0:T(8,128)(2,1)} copy(bf16[1,512,512]{2,1,0:T(8,128)(2,1)} %shard_map.82) | data formatting | bytes 1048576
